TPU v7x, 32 devices: a whole 2x2x4 slice. The times are simulated.
32 devices in a mesh: groups: 2 (over y), ctx: 4 (over z), head: 2 (over x), pair: 2 (over core).
Axes of the slice: x: 2, y: 2, z: 4, core: 2. Of those that a mesh axis runs over, the one named last changes fastest.
Arguments:
- student_query: bfloat16 [1024, 4096], P(('groups', 'ctx'), ('head', 'pair')), parts along dimension 0, may hold values from -25 to 25
- teacher_keys: bfloat16 [1024, 1024], P(('groups', 'ctx'), ('head', 'pair')), parts along dimension 0, may hold values from -9 to 9
- teacher_values: bfloat16 [1024, 1024], P(('groups', 'ctx'), ('head', 'pair')), parts along dimension 0, may hold values from -6 to 6
- band_span: int32 [1024], P(('groups', 'ctx')), parts along dimension 0, may hold values from 256 to 1024, as said below
- residual_in: bfloat16 [1024, 4096], P(('groups', 'ctx'), ('head', 'pair')), parts along dimension 0, may hold values from -3 to 3
- norm_gain: float32 [4096], replicated, may hold values from 0.25 to 1.75
- w_gate: bfloat16 [4096, 7168], P('ctx', ('head', 'pair')), may hold values from -0.09375 to 0.09375
- w_up: bfloat16 [4096, 7168], P('ctx', ('head', 'pair')), may hold values from -0.09375 to 0.09375
- w_down: bfloat16 [7168, 4096], P(('head', 'pair'), 'ctx'), may hold values from -0.0625 to 0.0625
- teacher_feats: bfloat16 [1024, 7168], P(('groups', 'ctx'), ('head', 'pair')), parts along dimension 0, may hold values from -31 to 31
- keep_tiles: int32 [1024, 56], P(('groups', 'ctx'), ('head', 'pair')), parts along dimension 0, may hold values from 0 to 1, as said below
Outputs:
- layer_out: bfloat16 [1024, 4096], P(('groups', 'ctx'), ('head', 'pair')), parts along dimension 0
- loss_value: float32 [2], P('groups'), parts along dimension 0
- grad_resid: float32 [1024, 4096], P(('groups', 'ctx'), ('head', 'pair')), parts along dimension 0
There are 2 independent parts, one for each index of `groups`. A program takes and returns all parts, laid end to end along the dimension named above; an argument that names none is the same for every part. Nothing has to cross between parts.
Inputs may be any that keep to these rules, and one draw needn't show every extreme that they name: `band_span`: some token's span equals 1024. `keep_tiles`: the first token keeps every tile.
All inputs are finite; a program needn't handle non-finite values.
Results may differ from a plain program's by a relative error of at most 0.014.
Values may be sent and summed in bfloat16 or wider, within the bound.
No kernel may reach another device: no remote copies, remote signals or barrier semaphores. Data moves between devices by JAX's collectives and lax.ppermute only.
A program may use at most 128 MiB of HBM per device.

v0:
```python
import math
import jax
import jax.numpy as jnp
from jax import lax
from jax.sharding import PartitionSpec as P

D = 4096
HEADS = 32
KV_HEADS = 8
HEAD_DIM = 128
TILE = 128
BAND = 8


def passed_along(block, axis, distance):
    devices = range(lax.axis_size(axis))
    route = [(i - distance, i) for i in devices if i - distance in devices]
    return lax.ppermute(block, axis, route)


def attend_heads(query_part, key_rows, value_rows, allowed):
    scores = jnp.einsum("thd,sd->hts", query_part, key_rows, preferred_element_type=jnp.float32) * (
        1.0 / math.sqrt(HEAD_DIM)
    )
    masked = jnp.where(allowed[None], scores, -jnp.inf)
    highest = jnp.max(masked, axis=-1, keepdims=True)
    weights = jnp.exp(masked - highest)
    normalized = (weights / jnp.sum(weights, axis=-1, keepdims=True)).astype(jnp.bfloat16)
    return jnp.einsum("hts,sd->thd", normalized, value_rows, preferred_element_type=jnp.float32)


def local(
    student_query,
    teacher_keys,
    teacher_values,
    band_span,
    residual_in,
    norm_gain,
    w_gate,
    w_up,
    w_down,
    teacher_feats,
    keep_tiles,
):
    tok_rows = student_query.shape[0]
    kv_local = teacher_keys.shape[1] // HEAD_DIM
    group_size = HEADS // KV_HEADS
    ctx_index = lax.axis_index("ctx")
    paired = jnp.stack([teacher_keys, teacher_values])

    def pass_block(carried, unused_step):
        moved = passed_along(carried, "ctx", 1)
        return (moved, moved)

    unused_last, earlier = lax.scan(pass_block, paired, None, length=BAND)
    all_blocks = jnp.concatenate([paired[None], earlier], axis=0)
    rounds_count = BAND + 1
    round_ids = jnp.arange(rounds_count, dtype=jnp.int32)
    key_pos = (
        (ctx_index - round_ids)[:, None] * tok_rows + jnp.arange(tok_rows, dtype=jnp.int32)[None, :]
    ).reshape(-1)
    query_pos = ctx_index * tok_rows + jnp.arange(tok_rows, dtype=jnp.int32)
    distance = query_pos[:, None] - key_pos[None, :]
    allowed = (distance >= 0) & (distance < band_span[:, None]) & (key_pos[None, :] >= 0)
    keys_flat = all_blocks[:, 0].reshape(rounds_count * tok_rows, kv_local, HEAD_DIM)
    values_flat = all_blocks[:, 1].reshape(rounds_count * tok_rows, kv_local, HEAD_DIM)
    query_heads = student_query.reshape(tok_rows, kv_local, group_size, HEAD_DIM)
    outputs = []
    for kv_head in range(kv_local):
        for first_head in range(0, group_size, 2):
            outputs.append(
                attend_heads(
                    query_heads[:, kv_head, first_head : first_head + 2],
                    keys_flat[:, kv_head],
                    values_flat[:, kv_head],
                    allowed,
                )
            )
    attended = jnp.concatenate(outputs, axis=1).reshape(tok_rows, -1)
    residual = (residual_in.astype(jnp.float32) + attended).astype(jnp.bfloat16)
    gathered = lax.all_gather(residual, ("head", "pair"), axis=1, tiled=True)
    full_float = gathered.astype(jnp.float32)
    rms_value = jnp.sqrt(jnp.mean(full_float * full_float, axis=1, keepdims=True) + 1e-05)
    normed = (full_float / rms_value * norm_gain).astype(jnp.bfloat16)
    gate_full, up_full = (
        lax.all_gather(w_gate, "ctx", axis=0, tiled=True),
        lax.all_gather(w_up, "ctx", axis=0, tiled=True),
    )
    gate_proj = jnp.dot(normed, gate_full, preferred_element_type=jnp.float32)
    up_proj = jnp.dot(normed, up_full, preferred_element_type=jnp.float32)
    lifted = jnp.maximum(gate_proj, 0.0)
    squared = lifted * lifted
    act_value = squared * up_proj
    hidden = act_value.astype(jnp.bfloat16)
    all_hidden = lax.all_gather(hidden, "ctx", axis=0, tiled=True)
    local_part = jnp.dot(all_hidden, w_down, preferred_element_type=jnp.float32).astype(
        jnp.bfloat16
    )
    routed = lax.all_to_all(local_part, "ctx", split_axis=0, concat_axis=1, tiled=True)
    down_sum = lax.psum_scatter(
        routed.astype(jnp.float32).astype(jnp.bfloat16),
        ("head", "pair"),
        scatter_dimension=1,
        tiled=True,
    ).astype(jnp.float32)
    resid_own = residual.astype(jnp.float32)
    layer_out = (resid_own + down_sum).astype(jnp.bfloat16)
    tile_count = keep_tiles.shape[1]
    keep_float = keep_tiles.astype(jnp.float32)
    keep_wide = jnp.broadcast_to(keep_float[:, :, None], (tok_rows, tile_count, TILE)).reshape(
        tok_rows, tile_count * TILE
    )
    differ = act_value - teacher_feats.astype(jnp.float32)
    loss_part = jnp.sum(keep_wide * differ * differ)
    count_part = jnp.sum(keep_float) * TILE
    loss_total, count_total = lax.psum((loss_part, count_part), ("ctx", "head", "pair"))
    loss_value = (loss_total / count_total).reshape(1)
    grad_act = keep_wide * differ
    grad_gate = (grad_act * up_proj * 2.0 * lifted).astype(jnp.bfloat16)
    grad_up = (grad_act * squared).astype(jnp.bfloat16)
    contract = (((1,), (1,)), ((), ()))
    grad_part = lax.dot_general(grad_gate, gate_full, contract, preferred_element_type=jnp.float32)
    grad_part = grad_part + lax.dot_general(
        grad_up, up_full, contract, preferred_element_type=jnp.float32
    )
    own_cols = residual.shape[1]
    own_start = lax.axis_index(("head", "pair")) * own_cols
    gain_own = lax.dynamic_slice_in_dim(norm_gain, own_start, own_cols, 0)
    rms_cubed = rms_value * rms_value * rms_value
    grad_norm = lax.psum_scatter(
        grad_part.astype(jnp.bfloat16), ("head", "pair"), scatter_dimension=1, tiled=True
    ).astype(jnp.float32)
    inner_sum = lax.psum(
        jnp.sum(gain_own * grad_norm * resid_own, axis=1, keepdims=True), ("head", "pair")
    )
    grad_resid = gain_own * grad_norm / rms_value - resid_own * inner_sum / (D * rms_cubed)
    return (layer_out, loss_value, grad_resid)


def solution(mesh):
    in_specs = (
        P(("groups", "ctx"), ("head", "pair")),
        P(("groups", "ctx"), ("head", "pair")),
        P(("groups", "ctx"), ("head", "pair")),
        P(("groups", "ctx")),
        P(("groups", "ctx"), ("head", "pair")),
        P(),
        P("ctx", ("head", "pair")),
        P("ctx", ("head", "pair")),
        P(("head", "pair"), "ctx"),
        P(("groups", "ctx"), ("head", "pair")),
        P(("groups", "ctx"), ("head", "pair")),
    )
    out_specs = (
        P(("groups", "ctx"), ("head", "pair")),
        P("groups"),
        P(("groups", "ctx"), ("head", "pair")),
    )
    return jax.shard_map(local, mesh=mesh, in_specs=in_specs, out_specs=out_specs, check_vma=False)
```

profile of v0, /device:TPU:0, one launch (start us, length us, event | category | flops | bytes accessed | tf_op | source)
XLA Modules:
  0.0 737.4 jit_solution(9024494652574293018)
XLA Ops:
  7.2 0.1 add_bitcast_fusion
  7.3 0.1 broadcast_compare_fusion
  7.4 0.9 fusion.71
  8.3 57.8 %while.12 = (s32[]{:T(128)}, bf16[2,128,256]{2,1,0:T(8,128)(2,1)S(1)}, bf16[8,2,128,256]{3,2,1,0:T(8,128)(2,1)S(1)}, s32[]{:T(128)}) while((s32[]{:T(128)}, bf16[2,128,256]{2,1,0:T(8,128)(2,1)S(1)}, bf16[8,2,128,256]{3,2,1,0:T(8,128)(2,1)S(1)}, s32[]{:T(128)}) %tuple.30), condition=%wide.region_1.2_spmd, body=%wide.region_0.1_spmd.sunk | while | flops 2 | bytes 1048681 | solution.py:55
  8.3 5.0 collective-permute-start
  13.3 2.7 collective-permute-done
  16.0 4.4 collective-permute-start
  20.4 2.5 collective-permute-done
  23.0 4.4 collective-permute-start
  27.4 2.5 collective-permute-done
  29.9 4.4 collective-permute-start
  34.3 2.5 collective-permute-done
  36.8 4.4 collective-permute-start
  41.2 3.5 collective-permute-done
  44.8 4.4 collective-permute-start
  49.2 3.0 collective-permute-done
  52.3 4.4 collective-permute-start
  56.7 2.5 collective-permute-done
  59.2 4.4 collective-permute-start
  63.6 2.5 collective-permute-done
  66.1 0.1 fusion.25
  66.2 0.1 reshape_squeeze.7
  66.4 0.9 fusion.76
  67.3 0.1 copy-done.4
  67.3 0.2 copy.24
  67.5 0.9 fusion.27
  68.4 0.6 fusion.80
  69.0 0.6 fusion.79
  69.6 0.6 fusion.78
  70.2 0.6 fusion.77
  70.8 0.1 reshape_squeeze.6
  70.9 0.9 fusion.75
  71.8 0.6 copy.42
  72.5 0.8 convolution_bitcast_fusion.3
  73.3 0.8 convolution_bitcast_fusion.2
  74.1 0.6 copy.46
  74.7 0.8 convolution_bitcast_fusion.1
  75.5 0.8 convolution_bitcast_fusion
  76.4 0.2 copy.35
  76.6 0.7 copy-done.5
  77.3 0.8 add_convert_fusion
  78.1 0.7 all-gather.7.cloned.1.call-update
  78.9 0.7 all-gather.9.cloned.1.call-update
  79.6 0.2 all-gather.11.cloned.1.call-start
  79.8 0.1 broadcast_in_dim.67
  79.9 0.3 copy.37
  80.2 16.9 %all-gather.5.cloned.1.call-done = bf16[128,4096]{1,0:T(8,128)(2,1)} async-done(((bf16[128,1024]{1,0:T(8,128)(2,1)}), bf16[128,4096]{1,0:T(8,128)(2,1)}) %all-gather.5.cloned.1.call-update) | async-done | bytes 1048592 | tf_op jit(solution)/shard_map/all_gather | solution.py:81
  97.1 1.5 fusion.21
  98.6 252.5 %all-gather.7.cloned.1.call-done = bf16[4096,1792]{1,0:T(8,128)(2,1)} async-done(((bf16[1024,1792]{1,0:T(8,128)(2,1)}), bf16[4096,1792]{1,0:T(8,128)(2,1)}) %all-gather.7.cloned.1.call-update) | async-done | bytes 14680080 | tf_op jit(solution)/shard_map/all_gather | solution.py:86
  351.1 7.7 %convolution_maximum_fusion = f32[128,1792]{1,0:T(8,128)S(1)} fusion(bf16[4096,1792]{1,0:T(8,128)(2,1)} %all-gather.7.cloned.1.call-done, bf16[128,4096]{1,0:T(8,128)(2,1)} %all-gather.5.cloned.1.call-done, f32[4096]{0:T(1024)S(1)} %copy-done.7, f32[128]{0:T(128)S(1)} %get-tuple-element.42), kind=kOutput, calls=%fused_computation.29 | convolution fusion | flops 1881374720 | bytes 16663040 | tf_op jit(solution)/shard_map/dot_general | solution.py:89
  358.9 244.5 %all-gather.9.cloned.1.call-done = bf16[4096,1792]{1,0:T(8,128)(2,1)} async-done(((bf16[1024,1792]{1,0:T(8,128)(2,1)}), bf16[4096,1792]{1,0:T(8,128)(2,1)}) %all-gather.9.cloned.1.call-update) | async-done | bytes 14680080 | tf_op jit(solution)/shard_map/all_gather | solution.py:87
  603.4 9.0 %multiply_reduce_fusion = (f32[]{:T(128)}, bf16[128,1792]{1,0:T(8,128)(2,1)}, f32[128,1792]{1,0:T(8,128)}) fusion(bf16[128,1792]{1,0:T(8,128)(2,1)S(1)} %copy-done.2, f32[128,1792]{1,0:T(8,128)S(1)} %copy.37, f32[128,1792]{1,0:T(8,128)S(1)} %convolution_maximum_fusion, bf16[4096,1792]{1,0:T(8,128)(2,1)} %all-gather.9.cloned.1.call-done, ...), kind=kOutput, calls=%fused_computation.46 | convolution fusion | flops 1882980352 | bytes 19415556 | tf_op jit(solution)/shard_map/dot_general | solution.py:90
  612.5 0.0 reduce-scatter.5.cloned.1.call-start
  612.5 10.8 %fusion.32 = f32[128,4096]{1,0:T(8,128)S(1)} fusion(bf16[4096,1792]{1,0:T(8,128)(2,1)} %all-gather.7.cloned.1.call-done, f32[128,1792]{1,0:T(8,128)} %copy-done.1, f32[128,1792]{1,0:T(8,128)} %get-tuple-element.43, f32[128,1792]{1,0:T(8,128)S(1)} %copy.37, bf16[128,1792]{1,0:T(8,128)(2,1)S(1)} %copy-done.2), kind=kOutput, calls=%fused_computation.66 | convolution fusion | flops 1881112576 | bytes 19988480 | tf_op jit(solution)/shard_map/dot_general | solution.py:122
  623.3 11.6 %fusion.4 = bf16[128,4096]{1,0:T(8,128)(2,1)} fusion(f32[128,4096]{1,0:T(8,128)S(1)} %fusion.32, bf16[4096,1792]{1,0:T(8,128)(2,1)} %all-gather.9.cloned.1.call-done, f32[128,1792]{1,0:T(8,128)} %copy-done.1, f32[128,1792]{1,0:T(8,128)S(1)} %copy.37, bf16[128,1792]{1,0:T(8,128)(2,1)S(1)} %copy-done.2, f32[128,1792]{1,0:T(8,128)} %get-tuple-element.43), kind=kOutput, calls=%fused_computation.6 | convolution fusion | flops 1881702400 | bytes 21037056 | tf_op jit(solution)/shard_map/dot_general | solution.py:123
  635.0 17.2 %all-gather.11.cloned.1.call-done = bf16[512,1792]{1,0:T(8,128)(2,1)} async-done(((bf16[128,1792]{1,0:T(8,128)(2,1)}), bf16[512,1792]{1,0:T(8,128)(2,1)}) %all-gather.11.cloned.1.call-update) | async-done | bytes 1835024 | tf_op jit(solution)/shard_map/all_gather | solution.py:95
  652.1 4.7 convolution_convert_fusion
  656.8 28.1 %all_to_all.19 = bf16[4,128,1024]{2,1,0:T(8,128)(2,1)S(1)} all-to-all(bf16[4,128,1024]{2,1,0:T(8,128)(2,1)S(1)} %bitcast.216), channel_id=1, replica_groups=mesh['groups'=2,'ctx'=4,'head'=2,'pair'=2] {'ctx'}, dimensions={0} | all-to-all | bytes 2097152 | tf_op jit(solution)/shard_map/all_to_all | solution.py:99
  684.9 1.1 copy.50
  686.1 0.6 convert_reduce_fusion
  687.3 31.7 %all-reduce = (f32[]{:T(128)}, f32[]{:T(128)}) all-reduce(f32[]{:T(128)} %get-tuple-element.29, f32[]{:T(128)S(6)} %mul.149), channel_id=1, replica_groups=mesh['groups'=2,'ctx'=4,'head'=2,'pair'=2] {'ctx','head','pair'}, use_global_device_ids=true, to_apply=%region_13.14 | all-reduce | flops 2 | bytes 16 | tf_op jit(solution)/shard_map/psum | solution.py:116
  720.4 1.1 fusion.29
  721.5 5.8 psum.23
  727.3 2.1 fusion.31
  (49 shorter events, 0.6 us)
Async XLA Ops:
  7.2 89.9 %all-gather.5.cloned.1.call-start = ((), (), s32[]{:S(2)}) async-start(), calls=%async_computation.3 | async-start | bytes 1310720 | tf_op jit(solution)/shard_map/all_gather | solution.py:81
  8.3 7.7 %collective-permute-start = (bf16[2,128,256]{2,1,0:T(8,128)(2,1)S(1)}, bf16[2,128,256]{2,1,0:T(8,128)(2,1)S(1)}, u32[]{:S(2)}, u32[]{:S(2)}) collective-permute-start(bf16[2,128,256]{2,1,0:T(8,128)(2,1)S(1)} %get-tuple-element.68), channel_id=1, source_target_pairs={{0,4},{4,8},{8,12},{1,5},{5,9},{9,13},{2,6},{6,10},{10,14},{3,7},{... | collective-permute-start | bytes 393224 | tf_op jit(solution)/shard_map/while/body/eval_jaxpr/ppermute | solution.py:18
  16.0 6.9 collective-permute-start
  23.0 6.9 collective-permute-start
  29.9 6.9 collective-permute-start
  36.8 7.9 %collective-permute-start = (bf16[2,128,256]{2,1,0:T(8,128)(2,1)S(1)}, bf16[2,128,256]{2,1,0:T(8,128)(2,1)S(1)}, u32[]{:S(2)}, u32[]{:S(2)}) collective-permute-start(bf16[2,128,256]{2,1,0:T(8,128)(2,1)S(1)} %get-tuple-element.68), channel_id=1, source_target_pairs={{0,4},{4,8},{8,12},{1,5},{5,9},{9,13},{2,6},{6,10},{10,14},{3,7},{... | collective-permute-start | bytes 393224 | tf_op jit(solution)/shard_map/while/body/eval_jaxpr/ppermute | solution.py:18
  44.8 7.4 %collective-permute-start = (bf16[2,128,256]{2,1,0:T(8,128)(2,1)S(1)}, bf16[2,128,256]{2,1,0:T(8,128)(2,1)S(1)}, u32[]{:S(2)}, u32[]{:S(2)}) collective-permute-start(bf16[2,128,256]{2,1,0:T(8,128)(2,1)S(1)} %get-tuple-element.68), channel_id=1, source_target_pairs={{0,4},{4,8},{8,12},{1,5},{5,9},{9,13},{2,6},{6,10},{10,14},{3,7},{... | collective-permute-start | bytes 393224 | tf_op jit(solution)/shard_map/while/body/eval_jaxpr/ppermute | solution.py:18
  52.3 6.9 collective-permute-start
  59.2 6.9 collective-permute-start
  66.4 1.0 copy-start.4
  66.4 1.1 copy-start.8
  76.3 1.0 copy-start.5
  78.1 273.1 %all-gather.7.cloned.1.call-start = ((), (), s32[]{:S(2)}) async-start(), calls=%async_computation.4 | async-start | bytes 18350080 | tf_op jit(solution)/shard_map/all_gather | solution.py:86
  78.8 1.0 copy-start.6
  78.8 524.6 %all-gather.9.cloned.1.call-start = ((), (), s32[]{:S(2)}) async-start(), calls=%async_computation.5 | async-start | bytes 18350080 | tf_op jit(solution)/shard_map/all_gather | solution.py:87
  79.6 572.6 %all-gather.11.cloned.1.call-start = ((), (), s32[]{:S(2)}) async-start(), calls=%async_computation.6 | async-start | bytes 2293760 | tf_op jit(solution)/shard_map/all_gather | solution.py:95
  79.9 271.2 %copy-start.7 = (f32[4096]{0:T(1024)S(1)}, f32[4096]{0:T(1024)}, u32[]{:S(2)}) copy-start(f32[4096]{0:T(1024)} %param.18) | copy-start | bytes 49156
  351.1 252.3 %copy-start.2 = (bf16[128,1792]{1,0:T(8,128)(2,1)S(1)}, bf16[128,1792]{1,0:T(8,128)(2,1)}, u32[]{:S(2)}) copy-start(bf16[128,1792]{1,0:T(8,128)(2,1)} %param.22) | copy-start | bytes 1376260
  351.1 252.3 %copy-start.3 = (bf16[128,4096]{1,0:T(8,128)(2,1)S(1)}, bf16[128,4096]{1,0:T(8,128)(2,1)}, u32[]{:S(2)}) copy-start(bf16[128,4096]{1,0:T(8,128)(2,1)} %all-gather.5.cloned.1.call-done) | copy-start | bytes 3145732
  358.9 253.6 %copy-start.1 = (f32[128,1792]{1,0:T(8,128)}, f32[128,1792]{1,0:T(8,128)S(1)}, u32[]{:S(2)}) copy-start(f32[128,1792]{1,0:T(8,128)S(1)} %convolution_maximum_fusion) | copy-start | bytes 2752516
  612.5 107.9 %reduce-scatter.5.cloned.1.call-start = ((), (), s32[]{:S(2)}) async-start(), calls=%async_computation.8 | async-start | bytes 1310720 | tf_op jit(solution)/shard_map/reduce_scatter | solution.py:130
  634.9 92.3 %reduce-scatter.3.cloned.1.call-start = ((), (), s32[]{:S(2)}) async-start(), calls=%async_computation.7 | async-start | bytes 1310720 | tf_op jit(solution)/shard_map/reduce_scatter | solution.py:100
  684.9 35.5 %copy-start = (bf16[128,1024]{1,0:T(8,128)(2,1)S(1)}, bf16[128,1024]{1,0:T(8,128)(2,1)}, u32[]{:S(2)}) copy-start(bf16[128,1024]{1,0:T(8,128)(2,1)} %add_convert_fusion) | copy-start | bytes 786436
Sparse Core Ops, SparseCore 0:
  78.2 18.8 all-gather.4
  98.6 252.4 all-gather.6
  352.7 250.6 all-gather.8
  612.6 39.5 all-gather.10
  654.5 23.6 reduce-scatter.4
  686.2 23.9 reduce-scatter.2
where the time goes:
time: 738 us; the launch traced here: 737 us
  waiting for transfers between devices  554 us (75%)
  blocking collectives  65.6 us (9%)
  matrix products  49.4 us (7%)
  starting transfers between devices  36 us (5%)
  between operations  17.5 us (2%)
  other arithmetic  8.21 us (1%)
    all_gather x1, waiting for transfers between devices, local(): lax.all_gather(w_gate, 'ctx', axis=0, tiled=True)  253 us
    all_gather x1, waiting for transfers between devices, local(): lax.all_gather(w_up, 'ctx', axis=0, tiled=True)  245 us
    ppermute x8, starting transfers between devices, passed_along(): return lax.ppermute(block, axis, route)  35.6 us
    psum x1, blocking collectives, local(): lax.psum((loss_part, count_part), ('ctx', 'head', 'pair'))  31.7 us
    all_to_all x1, blocking collectives, local(): lax.all_to_all(local_part, 'ctx', split_axis=0, concat_axis=1, tiled=True)  28.1 us
    ppermute x8, waiting for transfers between devices, passed_along(): return lax.ppermute(block, axis, route)  21.8 us
    all_gather x1, waiting for transfers between devices, local(): all_hidden = lax.all_gather(hidden, 'ctx', axis=0, tiled=True)  17.2 us
    all_gather x1, waiting for transfers between devices, local(): gathered = lax.all_gather(residual, ('head', 'pair'), axis=1, tiled=True)  16.9 us
  transfers between devices with their start and end apart: 14, of which 12 were waited for; matrix products, arithmetic and copies ran while one was open for 5% of the time, Pallas kernels for 0%

commit v1 on v0

--- a/solution.py
+++ b/solution.py
@@ -10,6 +10,13 @@
 HEAD_DIM = 128
 TILE = 128
 BAND = 8
+
+
+def gather_over(array, axis, dim):
+    size = lax.axis_size(axis)
+    blocks = jnp.stack([array for _ in range(size)])
+    blocks = lax.all_to_all(blocks, axis, split_axis=0, concat_axis=0)
+    return jnp.concatenate(blocks, axis=dim)
 
 
 def passed_along(block, axis, distance):
@@ -84,7 +91,7 @@
     normed = (full_float / rms_value * norm_gain).astype(jnp.bfloat16)
     gate_full, up_full = (
         lax.all_gather(w_gate, "ctx", axis=0, tiled=True),
-        lax.all_gather(w_up, "ctx", axis=0, tiled=True),
+        gather_over(w_up, "ctx", 0),
     )
     gate_proj = jnp.dot(normed, gate_full, preferred_element_type=jnp.float32)
     up_proj = jnp.dot(normed, up_full, preferred_element_type=jnp.float32)

time: 738 us -> 774 us (1.049)
  waiting for transfers between devices: 554 us -> 577 us
    all_gather x1, waiting for transfers between devices: 253 us -> 502 us  [local(): lax.all_gather(w_gate, 'ctx', axis=0, tiled=True)]
    all_gather x1 -> x0, waiting for transfers between devices: 245 us -> none  [local(): lax.all_gather(w_up, 'ctx', axis=0, tiled=True)]
    all_to_all x0 -> x1, waiting for transfers between devices: none -> 30.2 us  [gather_over(): blocks = lax.all_to_all(blocks, axis, split_axis=0, concat_axis=0)]
    all_gather x1, waiting for transfers between devices: 16.9 us -> 4.17 us  [local(): gathered = lax.all_gather(residual, ('head', 'pair'), axis=1, tiled=True)]
  transfers between devices with their start and end apart: 14 -> 14, of which waited for: 12 -> 12; matrix products, arithmetic and copies ran while one was open for 5% -> 6% of each run, Pallas kernels for 0% -> 0%
where the time goes in v1:
time: 774 us; the launch traced here: 773 us
  waiting for transfers between devices  577 us (75%)
  blocking collectives  65.6 us (8%)
  matrix products  49.3 us (6%)
  starting transfers between devices  42.8 us (6%)
  between operations  17.2 us (2%)
  local copies, waits for them, and re-layouts  12.6 us (2%)
  other arithmetic  8.21 us (1%)
    all_gather x1, waiting for transfers between devices, local(): lax.all_gather(w_gate, 'ctx', axis=0, tiled=True)  502 us
    ppermute x8, starting transfers between devices, passed_along(): return lax.ppermute(block, axis, route)  35.6 us
    psum x1, blocking collectives, local(): lax.psum((loss_part, count_part), ('ctx', 'head', 'pair'))  31.7 us
    all_to_all x1, waiting for transfers between devices, gather_over(): blocks = lax.all_to_all(blocks, axis, split_axis=0, concat_axis=0)  30.2 us
    all_to_all x1, blocking collectives, local(): lax.all_to_all(local_part, 'ctx', split_axis=0, concat_axis=1, tiled=True)  28.1 us
    ppermute x8, waiting for transfers between devices, passed_along(): return lax.ppermute(block, axis, route)  21.8 us
    all_gather x1, waiting for transfers between devices, local(): all_hidden = lax.all_gather(hidden, 'ctx', axis=0, tiled=True)  18 us
  transfers between devices with their start and end apart: 14, of which 12 were waited for; matrix products, arithmetic and copies ran while one was open for 6% of the time, Pallas kernels for 0%

profile of v1, /device:TPU:0, one launch (start us, length us, event | category | flops | bytes accessed | tf_op | source)
XLA Modules:
  0.0 773.1 jit_solution(7163228802819072010)
XLA Ops:
  7.2 0.1 add_bitcast_fusion
  7.3 0.1 broadcast_compare_fusion
  7.4 0.9 fusion.71
  8.3 57.8 %while.12 = (s32[]{:T(128)}, bf16[2,128,256]{2,1,0:T(8,128)(2,1)S(1)}, bf16[8,2,128,256]{3,2,1,0:T(8,128)(2,1)S(1)}, s32[]{:T(128)}) while((s32[]{:T(128)}, bf16[2,128,256]{2,1,0:T(8,128)(2,1)S(1)}, bf16[8,2,128,256]{3,2,1,0:T(8,128)(2,1)S(1)}, s32[]{:T(128)}) %tuple.30), condition=%wide.region_1.2_spmd, body=%wide.region_0.1_spmd.sunk | while | flops 2 | bytes 1048681 | solution.py:62
  8.3 5.0 collective-permute-start
  13.3 2.7 collective-permute-done
  16.0 4.4 collective-permute-start
  20.4 2.5 collective-permute-done
  23.0 4.4 collective-permute-start
  27.4 2.5 collective-permute-done
  29.9 4.4 collective-permute-start
  34.3 2.5 collective-permute-done
  36.8 4.4 collective-permute-start
  41.2 3.5 collective-permute-done
  44.8 4.4 collective-permute-start
  49.2 3.0 collective-permute-done
  52.3 4.4 collective-permute-start
  56.7 2.5 collective-permute-done
  59.2 4.4 collective-permute-start
  63.6 2.5 collective-permute-done
  66.1 0.1 fusion.25
  66.2 0.1 reshape_squeeze.7
  66.4 0.9 fusion.76
  67.3 0.1 copy-done.4
  67.3 0.2 copy.24
  67.5 0.9 fusion.27
  68.4 0.6 fusion.80
  69.0 0.6 fusion.79
  69.6 0.6 fusion.78
  70.2 0.6 fusion.77
  70.8 0.1 reshape_squeeze.6
  70.9 0.9 fusion.75
  71.8 0.6 copy.42
  72.5 0.8 convolution_bitcast_fusion.3
  73.3 0.8 convolution_bitcast_fusion.2
  74.1 0.6 copy.46
  74.7 0.8 convolution_bitcast_fusion.1
  75.5 0.8 convolution_bitcast_fusion
  76.4 0.2 copy.35
  76.6 0.7 copy-done.5
  77.3 0.8 add_convert_fusion
  78.1 0.7 all-gather.6.cloned.1.call-update
  78.8 6.6 stack.19
  85.4 6.8 all-to-all-start
  92.2 0.2 all-gather.8.cloned.1.call-start
  92.5 0.1 broadcast_in_dim.67
  92.6 0.3 copy.37
  92.9 4.2 all-gather.4.cloned.1.call-done
  97.1 1.5 fusion.21
  98.6 502.1 %all-gather.6.cloned.1.call-done = bf16[4096,1792]{1,0:T(8,128)(2,1)} async-done(((bf16[1024,1792]{1,0:T(8,128)(2,1)}), bf16[4096,1792]{1,0:T(8,128)(2,1)}) %all-gather.6.cloned.1.call-update) | async-done | bytes 14680080 | tf_op jit(solution)/shard_map/all_gather | solution.py:93
  600.7 7.7 convolution_maximum_fusion
  608.4 30.2 %all-to-all-done = bf16[4,1024,1792]{2,1,0:T(8,128)(2,1)} async-done(((bf16[4,1024,1792]{2,1,0:T(8,128)(2,1)}), bf16[4,1024,1792]{2,1,0:T(8,128)(2,1)}, u32[]{:S(2)}, u32[]{:S(2)}) %all-to-all-start) | async-done | bytes 14680096 | tf_op jit(solution)/shard_map/all_to_all | solution.py:18
  638.7 9.0 %multiply_reduce_fusion = (f32[]{:T(128)}, bf16[128,1792]{1,0:T(8,128)(2,1)}, f32[128,1792]{1,0:T(8,128)}) fusion(bf16[128,1792]{1,0:T(8,128)(2,1)S(1)} %copy-done.2, f32[128,1792]{1,0:T(8,128)S(1)} %copy.37, f32[128,1792]{1,0:T(8,128)S(1)} %convolution_maximum_fusion, bf16[4096,1792]{1,0:T(8,128)(2,1)} %bitcast.27, bf16[128,4096]{1,0:T(8,128)(2,1)S(1)} %copy-done.3, ...), kind=kOutput, calls=%fused_computation.46 | convolution fusion | flops 1882980352 | bytes 19415556 | tf_op jit(solution)/shard_map/dot_general | solution.py:97
  647.8 10.6 %fusion.32 = f32[128,4096]{1,0:T(8,128)S(1)} fusion(bf16[4096,1792]{1,0:T(8,128)(2,1)} %all-gather.6.cloned.1.call-done, f32[128,1792]{1,0:T(8,128)} %copy-done.1, f32[128,1792]{1,0:T(8,128)} %get-tuple-element.43, f32[128,1792]{1,0:T(8,128)S(1)} %copy.37, bf16[128,1792]{1,0:T(8,128)(2,1)S(1)} %copy-done.2), kind=kOutput, calls=%fused_computation.66 | convolution fusion | flops 1881112576 | bytes 19988480 | tf_op jit(solution)/shard_map/dot_general | solution.py:129
  658.4 11.6 %fusion.4 = bf16[128,4096]{1,0:T(8,128)(2,1)} fusion(f32[128,4096]{1,0:T(8,128)S(1)} %fusion.32, bf16[4096,1792]{1,0:T(8,128)(2,1)} %bitcast.27, f32[128,1792]{1,0:T(8,128)} %copy-done.1, f32[128,1792]{1,0:T(8,128)S(1)} %copy.37, bf16[128,1792]{1,0:T(8,128)(2,1)S(1)} %copy-done.2, f32[128,1792]{1,0:T(8,128)} %get-tuple-element.43), kind=kOutput, calls=%fused_computation.6 | convolution fusion | flops 1881702400 | bytes 21037056 | tf_op jit(solution)/shard_map/dot_general | solution.py:130
  670.1 18.0 %all-gather.8.cloned.1.call-done = bf16[512,1792]{1,0:T(8,128)(2,1)} async-done(((bf16[128,1792]{1,0:T(8,128)(2,1)}), bf16[512,1792]{1,0:T(8,128)(2,1)}) %all-gather.8.cloned.1.call-update) | async-done | bytes 1835024 | tf_op jit(solution)/shard_map/all_gather | solution.py:102
  688.1 4.7 convolution_convert_fusion
  692.8 28.1 %all_to_all.24 = bf16[4,128,1024]{2,1,0:T(8,128)(2,1)S(1)} all-to-all(bf16[4,128,1024]{2,1,0:T(8,128)(2,1)S(1)} %bitcast.217), channel_id=1, replica_groups=mesh['groups'=2,'ctx'=4,'head'=2,'pair'=2] {'ctx'}, dimensions={0} | all-to-all | bytes 2097152 | tf_op jit(solution)/shard_map/all_to_all | solution.py:106
  720.9 1.1 copy.50
  722.0 0.6 convert_reduce_fusion
  723.3 31.7 %all-reduce = (f32[]{:T(128)}, f32[]{:T(128)}) all-reduce(f32[]{:T(128)} %get-tuple-element.29, f32[]{:T(128)S(6)} %mul.149), channel_id=1, replica_groups=mesh['groups'=2,'ctx'=4,'head'=2,'pair'=2] {'ctx','head','pair'}, use_global_device_ids=true, to_apply=%region_13.14 | all-reduce | flops 2 | bytes 16 | tf_op jit(solution)/shard_map/psum | solution.py:123
  756.4 1.1 fusion.29
  757.5 5.8 psum.23
  763.3 2.1 fusion.31
  (49 shorter events, 0.6 us)
Async XLA Ops:
  7.2 89.9 %all-gather.4.cloned.1.call-start = ((), (), s32[]{:S(2)}) async-start(), calls=%async_computation.4 | async-start | bytes 1310720 | tf_op jit(solution)/shard_map/all_gather | solution.py:88
  8.3 7.7 collective-permute-start
  16.0 6.9 collective-permute-start
  23.0 6.9 collective-permute-start
  29.9 6.9 collective-permute-start
  36.8 7.9 %collective-permute-start = (bf16[2,128,256]{2,1,0:T(8,128)(2,1)S(1)}, bf16[2,128,256]{2,1,0:T(8,128)(2,1)S(1)}, u32[]{:S(2)}, u32[]{:S(2)}) collective-permute-start(bf16[2,128,256]{2,1,0:T(8,128)(2,1)S(1)} %get-tuple-element.68), channel_id=1, source_target_pairs={{0,4},{4,8},{8,12},{1,5},{5,9},{9,13},{2,6},{6,10},{10,14},{3,7},{... | collective-permute-start | bytes 393224 | tf_op jit(solution)/shard_map/while/body/eval_jaxpr/ppermute | solution.py:25
  44.8 7.4 collective-permute-start
  52.3 6.9 collective-permute-start
  59.2 6.9 collective-permute-start
  66.4 1.0 copy-start.4
  66.4 1.1 copy-start.8
  76.3 1.0 copy-start.5
  78.1 522.6 %all-gather.6.cloned.1.call-start = ((), (), s32[]{:S(2)}) async-start(), calls=%async_computation.5 | async-start | bytes 18350080 | tf_op jit(solution)/shard_map/all_gather | solution.py:93
  85.4 7.1 copy-start.6
  85.4 553.2 %all-to-all-start = ((bf16[4,1024,1792]{2,1,0:T(8,128)(2,1)}), bf16[4,1024,1792]{2,1,0:T(8,128)(2,1)}, u32[]{:S(2)}, u32[]{:S(2)}) async-start(bf16[4,1024,1792]{2,1,0:T(8,128)(2,1)} %stack.19), calls=%async_computation | async-start | bytes 29360128 | tf_op jit(solution)/shard_map/all_to_all | solution.py:18
  92.2 595.9 %all-gather.8.cloned.1.call-start = ((), (), s32[]{:S(2)}) async-start(), calls=%async_computation.6 | async-start | bytes 2293760 | tf_op jit(solution)/shard_map/all_gather | solution.py:102
  92.6 508.1 %copy-start.7 = (f32[4096]{0:T(1024)S(1)}, f32[4096]{0:T(1024)}, u32[]{:S(2)}) copy-start(f32[4096]{0:T(1024)} %param.18) | copy-start | bytes 49156
  600.7 38.0 %copy-start.2 = (bf16[128,1792]{1,0:T(8,128)(2,1)S(1)}, bf16[128,1792]{1,0:T(8,128)(2,1)}, u32[]{:S(2)}) copy-start(bf16[128,1792]{1,0:T(8,128)(2,1)} %param.22) | copy-start | bytes 1376260
  600.7 38.0 %copy-start.3 = (bf16[128,4096]{1,0:T(8,128)(2,1)S(1)}, bf16[128,4096]{1,0:T(8,128)(2,1)}, u32[]{:S(2)}) copy-start(bf16[128,4096]{1,0:T(8,128)(2,1)} %all-gather.4.cloned.1.call-done) | copy-start | bytes 3145732
  608.4 39.3 %copy-start.1 = (f32[128,1792]{1,0:T(8,128)}, f32[128,1792]{1,0:T(8,128)S(1)}, u32[]{:S(2)}) copy-start(f32[128,1792]{1,0:T(8,128)S(1)} %convolution_maximum_fusion) | copy-start | bytes 2752516
  647.7 108.7 %reduce-scatter.5.cloned.1.call-start = ((), (), s32[]{:S(2)}) async-start(), calls=%async_computation.8 | async-start | bytes 1310720 | tf_op jit(solution)/shard_map/reduce_scatter | solution.py:137
  670.1 93.2 %reduce-scatter.3.cloned.1.call-start = ((), (), s32[]{:S(2)}) async-start(), calls=%async_computation.7 | async-start | bytes 1310720 | tf_op jit(solution)/shard_map/reduce_scatter | solution.py:107
  720.9 35.5 %copy-start = (bf16[128,1024]{1,0:T(8,128)(2,1)S(1)}, bf16[128,1024]{1,0:T(8,128)(2,1)}, u32[]{:S(2)}) copy-start(bf16[128,1024]{1,0:T(8,128)(2,1)} %add_convert_fusion) | copy-start | bytes 786436
Sparse Core Ops, SparseCore 0:
  78.2 18.8 all-gather.3
  98.6 501.9 all-gather.5
  647.8 40.2 all-gather.7
  690.5 23.6 reduce-scatter.4
  722.1 23.9 reduce-scatter.2
